TPU v7x, 32 devices: a whole 2x2x4 slice. The times are simulated.
32 devices in a mesh: dp: 8 (over y, x, core), mp: 4 (over z).
Axes of the slice: x: 2, y: 2, z: 4, core: 2. Of those that a mesh axis runs over, the one named last changes fastest.
Arguments:
- tokens: bfloat16 [2, 8704, 1024], P(None, ('dp', 'mp')), may hold values from -6 to 6
- seg_ids: int32 [2, 8704], P(None, 'dp'), may hold values from 0 to 1, as said below
- qkv_weight: bfloat16 [3, 1024, 1024], P(None, 'dp', 'mp'), may hold values from -0.25 to 0.25
- qv_bias: bfloat16 [2, 1024], P(None, ('mp', 'dp')), may hold values from -2 to 2
- out_weight: bfloat16 [1024, 1024], P(('mp', 'dp')), may hold values from -0.1875 to 0.1875
- up_weight: bfloat16 [1024, 4096], P('dp', 'mp'), may hold values from -0.1875 to 0.1875
- up_bias: bfloat16 [4096], P(('mp', 'dp')), may hold values from -3 to 3
- down_weight: bfloat16 [4096, 1024], P(('mp', 'dp')), may hold values from -0.09375 to 0.09375
- norm_gain: bfloat16 [4, 1024], P(None, 'dp'), may hold values from 0.099609375 to 1.8984375
- norm_bias: bfloat16 [4, 1024], P(None, 'dp'), may hold values from -2 to 2
- branch_bias: bfloat16 [2, 1024], P(None, 'dp'), may hold values from -3 to 3
- out_grad: bfloat16 [2, 8704, 1024], P(None, ('dp', 'mp')), may hold values from -6 to 6
Outputs:
- layer_out: bfloat16 [2, 8704, 1024], P(None, ('dp', 'mp'))
- input_grad: float32 [2, 8704, 1024], P(None, ('dp', 'mp'))
- qkv_grad: float32 [3, 1024, 1024], P(None, 'dp', 'mp')
- qv_bias_grad: float32 [2, 1024], P(None, ('mp', 'dp'))
- out_weight_grad: float32 [1024, 1024], P(('mp', 'dp'))
- up_weight_grad: float32 [1024, 4096], P('dp', 'mp')
- up_bias_grad: float32 [4096], P(('mp', 'dp'))
- down_weight_grad: float32 [4096, 1024], P(('mp', 'dp'))
- norm_gain_grad: float32 [4, 1024], P(None, 'dp')
- norm_bias_grad: float32 [4, 1024], P(None, 'dp')
- branch_bias_grad: float32 [2, 1024], P(None, 'dp')
Inputs may be any that keep to these rules, and one draw needn't show every extreme that they name: `seg_ids`: each packed row of 1088 tokens holds 1 items numbered 0 upward in order, each of 1024 image codes plus 5 to 64 caption tokens; the rest of the row is padding numbered 1.
All inputs are finite; a program needn't handle non-finite values.
Results may differ from a plain program's by a relative error of at most 0.019.
Values may be sent and summed in bfloat16 or wider, within the bound.
A program may use at most 192 MiB of HBM per device.

v0:
```python
import math
import jax
import jax.numpy as jnp
from jax import lax
from jax.sharding import PartitionSpec as P

HEAD_DIM = 64
ALPHA = 32.0
EPS = 1e-05


def normalize(value, gain, shift):
    mean = jnp.mean(value, axis=-1, keepdims=True)
    centred = value - mean
    variance = jnp.mean(centred * centred, axis=-1, keepdims=True)
    return centred * lax.rsqrt(variance + EPS) * gain + shift


def normalize_back(value, gain, grad):
    mean = jnp.mean(value, axis=-1, keepdims=True)
    centred = value - mean
    variance = jnp.mean(centred * centred, axis=-1, keepdims=True)
    inverse = lax.rsqrt(variance + EPS)
    unit = centred * inverse
    scaled = grad * gain
    grad_in = inverse * (
        scaled
        - jnp.mean(scaled, axis=-1, keepdims=True)
        - unit * jnp.mean(scaled * unit, axis=-1, keepdims=True)
    )
    return (grad_in, jnp.sum(grad * unit, axis=0), jnp.sum(grad, axis=0))


def gelu_exact(value):
    return jax.nn.gelu(value, approximate=False)


def block_mask(seg_row, start, block):
    query_pos = start + jnp.arange(block, dtype=jnp.int32)
    key_pos = jnp.arange(seg_row.shape[0], dtype=jnp.int32)
    seg_block = seg_row[start : start + block]
    return (seg_block[:, None] == seg_row[None, :]) & (key_pos[None, :] <= query_pos[:, None])


def attend_forward(queries, keys, values, seg_row):
    length = queries.shape[0]
    block = length // 4
    results = []
    sums = []
    for part_index in range(4):
        start = part_index * block
        q_block = queries[start : start + block]
        allowed = block_mask(seg_row, start, block)[None]
        scores = jnp.einsum("qhd,khd->hqk", q_block, keys, preferred_element_type=jnp.float32)
        masked = jnp.where(allowed, scores, -1e30)
        top = jnp.max(masked, axis=-1, keepdims=True)
        expo = jnp.exp(ALPHA * (masked - top))
        total = jnp.sum(expo, axis=-1, keepdims=True)
        probs = (expo / total).astype(jnp.bfloat16)
        results.append(
            jnp.einsum("hqk,khd->qhd", probs, values, preferred_element_type=jnp.float32)
        )
        sums.append(ALPHA * top + jnp.log(total))
    return (jnp.concatenate(results, axis=0), jnp.concatenate(sums, axis=1))


def attend_backward(queries, keys, values, seg_row, log_sums, grad_out):
    length = queries.shape[0]
    block = length // 4
    grad_queries = []
    grad_keys = jnp.zeros(keys.shape, jnp.float32)
    grad_values = jnp.zeros(values.shape, jnp.float32)
    for part_index in range(4):
        start = part_index * block
        q_block = queries[start : start + block]
        g_block = grad_out[start : start + block]
        allowed = block_mask(seg_row, start, block)[None]
        scores = jnp.einsum("qhd,khd->hqk", q_block, keys, preferred_element_type=jnp.float32)
        masked = jnp.where(allowed, scores, -1e30)
        probs_full = jnp.exp(ALPHA * masked - log_sums[:, start : start + block])
        probs = probs_full.astype(jnp.bfloat16)
        grad_probs = jnp.einsum("qhd,khd->hqk", g_block, values, preferred_element_type=jnp.float32)
        delta = jnp.sum(probs_full * grad_probs, axis=-1, keepdims=True)
        grad_scores = (ALPHA * probs_full * (grad_probs - delta)).astype(jnp.bfloat16)
        grad_queries.append(
            jnp.einsum("hqk,khd->qhd", grad_scores, keys, preferred_element_type=jnp.float32)
        )
        grad_keys = grad_keys + jnp.einsum(
            "hqk,qhd->khd", grad_scores, q_block, preferred_element_type=jnp.float32
        )
        grad_values = grad_values + jnp.einsum(
            "hqk,qhd->khd", probs, g_block, preferred_element_type=jnp.float32
        )
    return (jnp.concatenate(grad_queries, axis=0), grad_keys, grad_values)


def on_device(
    tokens,
    seg_ids,
    qkv_weight,
    qv_bias,
    out_weight,
    up_weight,
    up_bias,
    down_weight,
    norm_gain,
    norm_bias,
    branch_bias,
    out_grad,
):

    def fetch():
        return (
            lax.all_gather(qkv_weight, "dp", axis=1, tiled=True),
            lax.all_gather(qv_bias, "dp", axis=1, tiled=True),
            lax.all_gather(out_weight, "dp", axis=0, tiled=True),
            lax.all_gather(up_weight, "dp", axis=0, tiled=True),
            lax.all_gather(up_bias, "dp", axis=0, tiled=True),
            lax.all_gather(down_weight, "dp", axis=0, tiled=True),
            lax.all_gather(norm_gain, "dp", axis=1, tiled=True),
            lax.all_gather(norm_bias, "dp", axis=1, tiled=True),
            lax.all_gather(branch_bias, "dp", axis=1, tiled=True),
        )

    scale = 1.0 / (ALPHA * math.sqrt(HEAD_DIM))
    batches = tokens.shape[0]
    length = seg_ids.shape[1]
    share = length // lax.axis_size("mp")
    saved = []
    outputs = []
    for step in range(batches):
        weights = fetch()
        qkv, qv_b, w_out, w_up, b_up, w_down, gains, shifts, branch_b = weights
        gains = gains.astype(jnp.float32)
        shifts = shifts.astype(jnp.float32)
        branch_b = branch_b.astype(jnp.float32)
        qv_b = qv_b.astype(jnp.float32)
        x_rows = tokens[step].astype(jnp.float32)
        seg_row = seg_ids[step]
        normed = normalize(x_rows, gains[0], shifts[0]).astype(jnp.bfloat16)
        hidden_in = lax.all_gather(normed, "mp", axis=0, tiled=True)
        queries = (
            (jnp.dot(hidden_in, qkv[0], preferred_element_type=jnp.float32) + qv_b[0]) * scale
        ).astype(jnp.bfloat16)
        keys = jnp.dot(hidden_in, qkv[1], preferred_element_type=jnp.float32).astype(jnp.bfloat16)
        values = (jnp.dot(hidden_in, qkv[2], preferred_element_type=jnp.float32) + qv_b[1]).astype(
            jnp.bfloat16
        )
        heads = queries.shape[1] // HEAD_DIM
        q_heads = queries.reshape(length, heads, HEAD_DIM)
        k_heads = keys.reshape(length, heads, HEAD_DIM)
        v_heads = values.reshape(length, heads, HEAD_DIM)
        attended, log_sums = attend_forward(q_heads, k_heads, v_heads, seg_row)
        mixed = attended.reshape(length, heads * HEAD_DIM).astype(jnp.bfloat16)

        def out_term(start, count, mixed=mixed, w_out=w_out):
            return jnp.dot(mixed, w_out, preferred_element_type=jnp.float32)

        branch = (
            lax.psum_scatter(
                out_term(jnp.int32(0), lax.axis_size("mp") * share).astype(jnp.bfloat16),
                "mp",
                scatter_dimension=0,
                tiled=True,
            ).astype(jnp.float32)
            + branch_b[0]
        )
        middle = x_rows + normalize(branch, gains[1], shifts[1])
        normed_two = normalize(middle, gains[2], shifts[2]).astype(jnp.bfloat16)
        hidden_two = lax.all_gather(normed_two, "mp", axis=0, tiled=True)
        pre = jnp.dot(hidden_two, w_up, preferred_element_type=jnp.float32) + b_up.astype(
            jnp.float32
        )
        act = gelu_exact(pre).astype(jnp.bfloat16)

        def ffn_term(start, count, act=act, w_down=w_down):
            return jnp.dot(act, w_down, preferred_element_type=jnp.float32)

        ffn_out = (
            lax.psum_scatter(
                ffn_term(jnp.int32(0), lax.axis_size("mp") * share).astype(jnp.bfloat16),
                "mp",
                scatter_dimension=0,
                tiled=True,
            ).astype(jnp.float32)
            + branch_b[1]
        )
        outputs.append((middle + normalize(ffn_out, gains[3], shifts[3])).astype(jnp.bfloat16))
        saved.append(
            (
                x_rows,
                hidden_in,
                q_heads,
                k_heads,
                v_heads,
                log_sums,
                mixed,
                branch,
                middle,
                hidden_two,
                pre,
                act,
                ffn_out,
            )
        )
    grad_inputs = []
    totals = None
    for step in range(batches):
        weights = fetch()
        qkv, qv_b, w_out, w_up, b_up, w_down, gains, shifts, branch_b = weights
        gains = gains.astype(jnp.float32)
        (
            x_rows,
            hidden_in,
            q_heads,
            k_heads,
            v_heads,
            log_sums,
            mixed,
            branch,
            middle,
            hidden_two,
            pre,
            act,
            ffn_out,
        ) = saved[step]
        seg_row = seg_ids[step]
        heads = q_heads.shape[1]
        grad_y = out_grad[step].astype(jnp.float32)
        grad_f, dgain_three, dshift_three = normalize_back(ffn_out, gains[3], grad_y)
        grad_f = grad_f.astype(jnp.bfloat16)
        dbranch_one = jnp.sum(grad_f.astype(jnp.float32), axis=0)
        pull = jax.vjp(gelu_exact, pre)[1]
        grad_f_all = lax.all_gather(grad_f, "mp", axis=0, tiled=True)
        dw_down = jnp.einsum("tf,td->fd", act, grad_f_all, preferred_element_type=jnp.float32)
        grad_act = jnp.einsum("td,fd->tf", grad_f_all, w_down, preferred_element_type=jnp.float32)
        grad_pre = pull(grad_act)[0].astype(jnp.bfloat16)
        dup_bias = jnp.sum(grad_pre.astype(jnp.float32), axis=0)
        dw_up = jnp.einsum("td,tf->df", hidden_two, grad_pre, preferred_element_type=jnp.float32)

        def ffn_back(start, count, grad_pre=grad_pre, w_up=w_up):
            return jnp.einsum("tf,df->td", grad_pre, w_up, preferred_element_type=jnp.float32)

        grad_norm_two = lax.psum_scatter(
            ffn_back(jnp.int32(0), lax.axis_size("mp") * share).astype(jnp.bfloat16),
            "mp",
            scatter_dimension=0,
            tiled=True,
        ).astype(jnp.float32)
        back_two, dgain_two, dshift_two = normalize_back(middle, gains[2], grad_norm_two)
        grad_mid = grad_y + back_two
        grad_branch, dgain_one, dshift_one = normalize_back(branch, gains[1], grad_mid)
        grad_branch = grad_branch.astype(jnp.bfloat16)
        dbranch_zero = jnp.sum(grad_branch.astype(jnp.float32), axis=0)
        grad_branch_all = lax.all_gather(grad_branch, "mp", axis=0, tiled=True)
        dw_out = jnp.einsum("tc,td->cd", mixed, grad_branch_all, preferred_element_type=jnp.float32)
        grad_mixed = jnp.einsum(
            "td,cd->tc", grad_branch_all, w_out, preferred_element_type=jnp.float32
        ).astype(jnp.bfloat16)
        grad_q, grad_k, grad_v = attend_backward(
            q_heads,
            k_heads,
            v_heads,
            seg_row,
            log_sums,
            grad_mixed.reshape(length, heads, HEAD_DIM),
        )
        grad_q = grad_q.reshape(length, heads * HEAD_DIM).astype(jnp.bfloat16)
        grad_k = grad_k.reshape(length, heads * HEAD_DIM).astype(jnp.bfloat16)
        grad_v = grad_v.reshape(length, heads * HEAD_DIM).astype(jnp.bfloat16)
        dw_qkv = jnp.stack(
            [
                scale
                * jnp.einsum("td,tc->dc", hidden_in, grad_q, preferred_element_type=jnp.float32),
                jnp.einsum("td,tc->dc", hidden_in, grad_k, preferred_element_type=jnp.float32),
                jnp.einsum("td,tc->dc", hidden_in, grad_v, preferred_element_type=jnp.float32),
            ]
        )
        dqv_bias = jnp.stack(
            [
                scale * jnp.sum(grad_q.astype(jnp.float32), axis=0),
                jnp.sum(grad_v.astype(jnp.float32), axis=0),
            ]
        )

        def attn_back(start, count, grad_q=grad_q, grad_k=grad_k, grad_v=grad_v, qkv=qkv):
            term = scale * jnp.einsum(
                "tc,dc->td", grad_q, qkv[0], preferred_element_type=jnp.float32
            )
            term = term + jnp.einsum(
                "tc,dc->td", grad_k, qkv[1], preferred_element_type=jnp.float32
            )
            return term + jnp.einsum(
                "tc,dc->td", grad_v, qkv[2], preferred_element_type=jnp.float32
            )

        grad_norm_one = lax.psum_scatter(
            attn_back(jnp.int32(0), lax.axis_size("mp") * share).astype(jnp.bfloat16),
            "mp",
            scatter_dimension=0,
            tiled=True,
        ).astype(jnp.float32)
        back_one, dgain_zero, dshift_zero = normalize_back(x_rows, gains[0], grad_norm_one)
        grad_inputs.append(grad_mid + back_one)
        local = (
            dw_qkv,
            dqv_bias,
            dw_out,
            dw_up,
            dup_bias,
            dw_down,
            jnp.stack([dgain_zero, dgain_one, dgain_two, dgain_three]),
            jnp.stack([dshift_zero, dshift_one, dshift_two, dshift_three]),
            jnp.stack([dbranch_zero, dbranch_one]),
        )
        local = (
            lax.psum_scatter(local[0], "dp", scatter_dimension=1, tiled=True),
            lax.psum_scatter(local[1], "dp", scatter_dimension=1, tiled=True),
            lax.psum_scatter(local[2], "dp", scatter_dimension=0, tiled=True),
            lax.psum_scatter(local[3], "dp", scatter_dimension=0, tiled=True),
            lax.psum_scatter(local[4], "dp", scatter_dimension=0, tiled=True),
            lax.psum_scatter(local[5], "dp", scatter_dimension=0, tiled=True),
            lax.psum_scatter(local[6], "dp", scatter_dimension=1, tiled=True),
            lax.psum_scatter(local[7], "dp", scatter_dimension=1, tiled=True),
            lax.psum_scatter(local[8], "dp", scatter_dimension=1, tiled=True),
        )
        totals = (
            local if totals is None else tuple((left + right for left, right in zip(totals, local)))
        )
    vectors = lax.psum((totals[6], totals[7], totals[8]), "mp")
    return (
        jnp.stack(outputs),
        jnp.stack(grad_inputs),
        totals[0],
        totals[1],
        totals[2],
        totals[3],
        totals[4],
        totals[5],
        vectors[0],
        vectors[1],
        vectors[2],
    )


def solution(mesh):
    in_specs = (
        P(None, ("dp", "mp"), None),
        P(None, "dp"),
        P(None, "dp", "mp"),
        P(None, ("mp", "dp")),
        P(("mp", "dp"), None),
        P("dp", "mp"),
        P(("mp", "dp")),
        P(("mp", "dp"), None),
        P(None, "dp"),
        P(None, "dp"),
        P(None, "dp"),
        P(None, ("dp", "mp"), None),
    )
    out_specs = (
        P(None, ("dp", "mp"), None),
        P(None, ("dp", "mp"), None),
        P(None, "dp", "mp"),
        P(None, ("mp", "dp")),
        P(("mp", "dp"), None),
        P("dp", "mp"),
        P(("mp", "dp")),
        P(("mp", "dp"), None),
        P(None, "dp"),
        P(None, "dp"),
        P(None, "dp"),
    )
    return jax.shard_map(
        on_device, mesh=mesh, in_specs=in_specs, out_specs=out_specs, check_vma=False
    )
```

profile of v0, /device:TPU:0, one launch (start us, length us, event | category | flops | bytes accessed | tf_op | source)
XLA Modules:
  0.0 1328.8 jit_solution(9125537895247549174)
XLA Ops:
  8.0 10.5 all_gather.34
  18.4 8.7 all_gather.35
  34.5 7.9 all-gather
  42.6 10.7 all_gather.75
  53.9 3.3 fusion.112
  57.2 31.6 %all-gather.24.cloned.1.call-done = bf16[1088,1024]{1,0:T(8,128)(2,1)} async-done(((bf16[272,1024]{1,0:T(8,128)(2,1)}), bf16[1088,1024]{1,0:T(8,128)(2,1)}) %all-gather.24.cloned.1.call-update) | async-done | bytes 2228240 | tf_op jit(solution)/shard_map/all_gather | solution.py:141
  88.9 3.3 convolution_convert_fusion.8
  93.5 2.6 fusion.39
  102.0 36.2 %all-gather.14.cloned.1.call-done = bf16[1088,1024]{1,0:T(8,128)(2,1)} async-done(((bf16[272,1024]{1,0:T(8,128)(2,1)}), bf16[1088,1024]{1,0:T(8,128)(2,1)}) %all-gather.14.cloned.1.call-update) | async-done | bytes 2228240 | tf_op jit(solution)/shard_map/all_gather | solution.py:141
  146.4 3.2 fusion.37
  151.0 2.7 fusion.36
  153.9 3.5 convolution_convert_fusion.9
  158.8 2.4 fusion.220
  208.6 8.9 all_gather.76
  217.5 13.4 %reduce-scatter.25.cloned.1.call-done = bf16[272,1024]{1,0:T(8,128)(2,1)} async-done(((bf16[1088,1024]{1,0:T(8,128)(2,1)}), bf16[272,1024]{1,0:T(8,128)(2,1)}) %reduce-scatter.25.cloned.1.call-update) | async-done | bytes 557072 | tf_op jit(solution)/shard_map/reduce_scatter | solution.py:160
  232.2 46.3 %reduce-scatter.29.cloned.1.call-done = bf16[272,1024]{1,0:T(8,128)(2,1)} async-done(((bf16[1088,1024]{1,0:T(8,128)(2,1)}), bf16[272,1024]{1,0:T(8,128)(2,1)}) %reduce-scatter.29.cloned.1.call-update) | async-done | bytes 557072 | tf_op jit(solution)/shard_map/reduce_scatter | solution.py:160
  286.6 8.7 all-gather.1
  295.4 12.3 all-gather.20.cloned.1.call-done
  307.7 50.5 %all-gather.18.cloned.1.call-done = bf16[1088,1024]{1,0:T(8,128)(2,1)} async-done(((bf16[272,1024]{1,0:T(8,128)(2,1)}), bf16[1088,1024]{1,0:T(8,128)(2,1)}) %all-gather.18.cloned.1.call-update) | async-done | bytes 2228240 | tf_op jit(solution)/shard_map/all_gather | solution.py:170
  358.2 15.7 %multiply_convert_fusion.9 = (bf16[1088,1024]{1,0:T(8,128)(2,1)}, f32[1088,1024]{1,0:T(8,128)}, f32[1088,1024]{1,0:T(8,128)}) fusion(f32[1024]{0:T(1024)S(1)} %bitcast.598, bf16[1088,1024]{1,0:T(8,128)(2,1)} %all-gather.18.cloned.1.call-done, bf16[1024,1024]{1,0:T(8,128)(2,1)} %all-gather.20.cloned.1.call-done), kind=kOutput, calls=%fused_computation.77 | convolution fusion | flops 2355232768 | bytes 15470592 | tf_op jit(solution)/shard_map/dot_general | solution.py:171
  373.8 13.0 all-gather.22.cloned.1.call-done
  386.8 6.2 convolution_convert_fusion.4
  393.3 43.5 %all-gather.26.cloned.1.call-done = bf16[1088,1024]{1,0:T(8,128)(2,1)} async-done(((bf16[272,1024]{1,0:T(8,128)(2,1)}), bf16[1088,1024]{1,0:T(8,128)(2,1)}) %all-gather.26.cloned.1.call-update) | async-done | bytes 2228240 | tf_op jit(solution)/shard_map/all_gather | solution.py:170
  436.7 15.5 %multiply_convert_fusion.8 = (bf16[1088,1024]{1,0:T(8,128)(2,1)S(1)}, f32[1088,1024]{1,0:T(8,128)}, f32[1088,1024]{1,0:T(8,128)}) fusion(f32[1024]{0:T(1024)S(1)} %bitcast.599, bf16[1088,1024]{1,0:T(8,128)(2,1)} %all-gather.26.cloned.1.call-done, bf16[1024,1024]{1,0:T(8,128)(2,1)} %all-gather.20.cloned.1.call-done), kind=kOutput, calls=%fused_computation.64 | convolution fusion | flops 2355232768 | bytes 15470592 | tf_op jit(solution)/shard_map/dot_general | solution.py:171
  453.6 3.9 convolution_convert_fusion.2
  457.6 26.2 %reduce-scatter.27.cloned.1.call-done = bf16[272,1024]{1,0:T(8,128)(2,1)} async-done(((bf16[1088,1024]{1,0:T(8,128)(2,1)}), bf16[272,1024]{1,0:T(8,128)(2,1)}) %reduce-scatter.27.cloned.1.call-update) | async-done | bytes 557072 | tf_op jit(solution)/shard_map/reduce_scatter | solution.py:180
  485.0 46.5 %reduce-scatter.31.cloned.1.call-done = bf16[272,1024]{1,0:T(8,128)(2,1)} async-done(((bf16[1088,1024]{1,0:T(8,128)(2,1)}), bf16[272,1024]{1,0:T(8,128)(2,1)}) %reduce-scatter.31.cloned.1.call-update) | async-done | bytes 557072 | tf_op jit(solution)/shard_map/reduce_scatter | solution.py:180
  534.6 3.0 fusion.154
  537.7 2.4 convert_reduce_fusion.14
  541.3 46.7 %all-gather.28.cloned.1.call-done = bf16[1088,1024]{1,0:T(8,128)(2,1)} async-done(((bf16[272,1024]{1,0:T(8,128)(2,1)}), bf16[1088,1024]{1,0:T(8,128)(2,1)}) %all-gather.28.cloned.1.call-update) | async-done | bytes 2228240 | tf_op jit(solution)/shard_map/all_gather | solution.py:234
  588.0 9.4 convert_reduce_fusion.1
  598.8 3.9 convolution_convert_fusion.1
  602.7 34.0 %all-gather.32.cloned.1.call-done = bf16[1088,1024]{1,0:T(8,128)(2,1)} async-done(((bf16[272,1024]{1,0:T(8,128)(2,1)}), bf16[1088,1024]{1,0:T(8,128)(2,1)}) %all-gather.32.cloned.1.call-update) | async-done | bytes 2228240 | tf_op jit(solution)/shard_map/all_gather | solution.py:234
  636.8 9.4 convert_reduce_fusion
  647.5 3.9 convolution_convert_fusion
  651.6 32.2 %reduce-scatter.33.cloned.1.call-done = bf16[272,1024]{1,0:T(8,128)(2,1)} async-done(((bf16[1088,1024]{1,0:T(8,128)(2,1)}), bf16[272,1024]{1,0:T(8,128)(2,1)}) %reduce-scatter.33.cloned.1.call-update) | async-done | bytes 557072 | tf_op jit(solution)/shard_map/reduce_scatter | solution.py:244
  683.8 47.6 %reduce-scatter.37.cloned.1.call-done = bf16[272,1024]{1,0:T(8,128)(2,1)} async-done(((bf16[1088,1024]{1,0:T(8,128)(2,1)}), bf16[272,1024]{1,0:T(8,128)(2,1)}) %reduce-scatter.37.cloned.1.call-update) | async-done | bytes 557072 | tf_op jit(solution)/shard_map/reduce_scatter | solution.py:244
  731.4 5.0 fusion.168
  736.5 2.7 multiply_reduce_fusion.9
  742.8 46.9 %all-gather.30.cloned.1.call-done = bf16[1088,1024]{1,0:T(8,128)(2,1)} async-done(((bf16[272,1024]{1,0:T(8,128)(2,1)}), bf16[1088,1024]{1,0:T(8,128)(2,1)}) %all-gather.30.cloned.1.call-update) | async-done | bytes 2228240 | tf_op jit(solution)/shard_map/all_gather | solution.py:255
  789.7 2.4 convolution_convert_fusion.7
  792.3 4.1 multiply_reduce_fusion.7
  802.5 35.8 %all-gather.34.cloned.1.call-done = bf16[1088,1024]{1,0:T(8,128)(2,1)} async-done(((bf16[272,1024]{1,0:T(8,128)(2,1)}), bf16[1088,1024]{1,0:T(8,128)(2,1)}) %all-gather.34.cloned.1.call-update) | async-done | bytes 2228240 | tf_op jit(solution)/shard_map/all_gather | solution.py:255
  847.9 4.1 multiply_reduce_fusion.6
  852.1 3.5 convolution_add_fusion.18
  880.9 4.3 multiply_reduce_fusion
  905.4 2.5 fusion.229
  908.0 2.5 convolution_add_fusion.15
  924.3 7.3 fusion.232
  936.7 35.9 %reduce-scatter.39.cloned.1.call-done = bf16[272,1024]{1,0:T(8,128)(2,1)} async-done(((bf16[1088,1024]{1,0:T(8,128)(2,1)}), bf16[272,1024]{1,0:T(8,128)(2,1)}) %reduce-scatter.39.cloned.1.call-update) | async-done | bytes 557072 | tf_op jit(solution)/shard_map/reduce_scatter | solution.py:297
  977.5 8.4 convolution_add_fusion.22
  986.0 5.5 fusion.231
  991.5 4.5 convolution_add_fusion.23
  997.1 2.6 fusion.230
  1001.9 2.7 convolution_bitcast_fusion
  1014.3 13.5 %all-reduce = f32[1024]{0:T(1024)S(1)} all-reduce(f32[1024]{0:T(1024)S(1)} %add.574), channel_id=23, replica_groups=mesh['dp'=8,'mp'=4] {'dp'}, use_global_device_ids=true, to_apply=%region_77.78.clone | all-reduce | flops 1024 | bytes 8192
  1031.6 14.8 %reduce-scatter.49.cloned.1.call-done = f32[32,2]{1,0:T(8,128)} async-done(((f32[256,2]{1,0:T(8,128)}), f32[32,2]{1,0:T(8,128)}) %reduce-scatter.49.cloned.1.call-update) | async-done | bytes 272
  1051.5 32.2 %reduce-scatter.51.cloned.1.call-done = f32[128,4]{1,0:T(8,128)} async-done(((f32[1024,4]{1,0:T(8,128)}), f32[128,4]{1,0:T(8,128)}) %reduce-scatter.51.cloned.1.call-update) | async-done | bytes 2064
  1084.5 36.7 %reduce-scatter.53.cloned.1.call-done = f32[128,4]{1,0:T(8,128)} async-done(((f32[1024,4]{1,0:T(8,128)}), f32[128,4]{1,0:T(8,128)}) %reduce-scatter.53.cloned.1.call-update) | async-done | bytes 2064
  1122.1 12.4 all-reduce.1
  1134.5 41.8 %reduce-scatter.47.cloned.1.call-done = f32[128,1024]{1,0:T(8,128)} async-done(((f32[1024,1024]{1,0:T(8,128)}), f32[128,1024]{1,0:T(8,128)}) %reduce-scatter.47.cloned.1.call-update) | async-done | bytes 524304 | tf_op jit(solution)/shard_map/reduce_scatter | solution.py:322
  1176.3 55.7 %reduce-scatter.45.cloned.1.call-done = f32[128,1024]{1,0:T(8,128)} async-done(((f32[1024,1024]{1,0:T(8,128)}), f32[128,1024]{1,0:T(8,128)}) %reduce-scatter.45.cloned.1.call-update) | async-done | bytes 524304 | tf_op jit(solution)/shard_map/reduce_scatter | solution.py:320
  1232.0 39.7 %reduce-scatter.43.cloned.1.call-done = f32[32,1024]{1,0:T(8,128)} async-done(((f32[256,1024]{1,0:T(8,128)}), f32[32,1024]{1,0:T(8,128)}) %reduce-scatter.43.cloned.1.call-update) | async-done | bytes 131088 | tf_op jit(solution)/shard_map/reduce_scatter | solution.py:319
  1271.7 50.0 %reduce-scatter.41.cloned.1.call-done = f32[3,128,256]{2,1,0:T(8,128)} async-done(((f32[3,1024,256]{2,1,0:T(8,128)}), f32[3,128,256]{2,1,0:T(8,128)}) %reduce-scatter.41.cloned.1.call-update) | async-done | bytes 393232 | tf_op jit(solution)/shard_map/reduce_scatter | solution.py:317
  (647 shorter events, 203.6 us)
Async XLA Ops:
  7.2 25.0 %copy-start.12 = (bf16[2,272,1024]{2,1,0:T(8,128)(2,1)S(1)}, bf16[2,272,1024]{2,1,0:T(8,128)(2,1)}, u32[]{:S(2)}) copy-start(bf16[2,272,1024]{2,1,0:T(8,128)(2,1)} %param.12) | copy-start | bytes 3342340
  7.2 50.0 %all-gather.16.cloned.1.call-start = ((), (), s32[]{:S(2)}) async-start(), calls=%async_computation.17 | async-start | bytes 1769472 | tf_op jit(solution)/shard_map/all_gather | solution.py:114
  7.9 81.0 %all-gather.24.cloned.1.call-start = ((), (), s32[]{:S(2)}) async-start(), calls=%async_computation.23 | async-start | bytes 2785280 | tf_op jit(solution)/shard_map/all_gather | solution.py:141
  28.6 13.9 %copy-start.110 = (s32[2,1088]{1,0:T(2,128)S(1)}, s32[2,1088]{1,0:T(2,128)}, u32[]{:S(2)}) copy-start(s32[2,1088]{1,0:T(2,128)} %param.13) | copy-start | bytes 26116
  28.6 14.0 %copy-start.88 = (bf16[32,1024]{1,0:T(8,128)(2,1)S(1)}, bf16[32,1024]{1,0:T(8,128)(2,1)}, u32[]{:S(2)}) copy-start(bf16[32,1024]{1,0:T(8,128)(2,1)} %param.16) | copy-start | bytes 196612
  33.7 104.5 %all-gather.14.cloned.1.call-start = ((), (), s32[]{:S(2)}) async-start(), calls=%async_computation.16 | async-start | bytes 2785280 | tf_op jit(solution)/shard_map/all_gather | solution.py:141
  34.4 196.5 %reduce-scatter.25.cloned.1.call-start = ((), (), s32[]{:S(2)}) async-start(), calls=%async_computation.18 | async-start | bytes 2785280 | tf_op jit(solution)/shard_map/reduce_scatter | solution.py:160
  53.9 39.6 %copy-start.152 = (f32[1,256]{1,0:T(1,128)}, f32[1,256]{1,0:T(1,128)S(1)}, u32[]{:S(2)}) copy-start(f32[1,256]{1,0:T(1,128)S(1)} %get-tuple-element.151) | copy-start | bytes 3076
  57.2 36.3 %copy-start.32 = (bf16[3,1024,256]{2,1,0:T(8,128)(2,1)S(1)}, bf16[3,1024,256]{2,1,0:T(8,128)(2,1)}, u32[]{:S(2)}) copy-start(bf16[3,1024,256]{2,1,0:T(8,128)(2,1)} %all-gather.16.cloned.1.call-done) | copy-start | bytes 4718596
  93.5 101.6 %copy-start.8 = (bf16[1088,256]{0,1:T(8,128)(2,1)}, bf16[1088,256]{0,1:T(8,128)(2,1)S(1)}, u32[]{:S(2)}) copy-start(bf16[1088,256]{0,1:T(8,128)(2,1)S(1)} %copy.138) | copy-start | bytes 1671172
  151.0 51.3 %copy-start.20 = (bf16[1088,256]{0,1:T(8,128)(2,1)}, bf16[1088,256]{0,1:T(8,128)(2,1)S(1)}, u32[]{:S(2)}) copy-start(bf16[1088,256]{0,1:T(8,128)(2,1)S(1)} %copy.136) | copy-start | bytes 1671172
  153.9 25.1 %copy-start.22 = (bf16[1088,256]{0,1:T(8,128)(2,1)}, bf16[1088,256]{0,1:T(8,128)(2,1)S(1)}, u32[]{:S(2)}) copy-start(bf16[1088,256]{0,1:T(8,128)(2,1)S(1)} %copy.130) | copy-start | bytes 1671172
  158.8 18.0 %copy-start.10 = (bf16[1088,256]{0,1:T(8,128)(2,1)}, bf16[1088,256]{0,1:T(8,128)(2,1)S(1)}, u32[]{:S(2)}) copy-start(bf16[1088,256]{0,1:T(8,128)(2,1)S(1)} %copy.132) | copy-start | bytes 1671172
  186.0 92.6 %reduce-scatter.29.cloned.1.call-start = ((), (), s32[]{:S(2)}) async-start(), calls=%async_computation.24 | async-start | bytes 2785280 | tf_op jit(solution)/shard_map/reduce_scatter | solution.py:160
  207.9 73.6 %copy-start.93 = (f32[1,1024]{1,0:T(1,128)S(1)}, f32[1,1024]{1,0:T(1,128)}, u32[]{:S(2)}) copy-start(f32[1,1024]{1,0:T(1,128)} %get-tuple-element.129) | copy-start | bytes 12292
  207.9 73.6 %copy-start.147 = (f32[1,1024]{1,0:T(1,128)S(1)}, f32[1,1024]{1,0:T(1,128)}, u32[]{:S(2)}) copy-start(f32[1,1024]{1,0:T(1,128)} %get-tuple-element.133) | copy-start | bytes 12292
  208.0 99.7 %all-gather.20.cloned.1.call-start = ((), (), s32[]{:S(2)}) async-start(), calls=%async_computation.20 | async-start | bytes 2359296 | tf_op jit(solution)/shard_map/all_gather | solution.py:117
  208.6 149.6 %all-gather.18.cloned.1.call-start = ((), (), s32[]{:S(2)}) async-start(), calls=%async_computation.19 | async-start | bytes 2785280 | tf_op jit(solution)/shard_map/all_gather | solution.py:170
  285.8 101.0 %all-gather.22.cloned.1.call-start = ((), (), s32[]{:S(2)}) async-start(), calls=%async_computation.21 | async-start | bytes 2359296 | tf_op jit(solution)/shard_map/all_gather | solution.py:119
  286.5 150.2 %all-gather.26.cloned.1.call-start = ((), (), s32[]{:S(2)}) async-start(), calls=%async_computation.25 | async-start | bytes 2785280 | tf_op jit(solution)/shard_map/all_gather | solution.py:170
  295.3 188.4 %reduce-scatter.27.cloned.1.call-start = ((), (), s32[]{:S(2)}) async-start(), calls=%async_computation.22 | async-start | bytes 2785280 | tf_op jit(solution)/shard_map/reduce_scatter | solution.py:180
  393.0 138.5 %reduce-scatter.31.cloned.1.call-start = ((), (), s32[]{:S(2)}) async-start(), calls=%async_computation.26 | async-start | bytes 2785280 | tf_op jit(solution)/shard_map/reduce_scatter | solution.py:180
  436.7 16.9 %copy-start.161 = (bf16[1024,1024]{1,0:T(8,128)(2,1)S(1)}, bf16[1024,1024]{1,0:T(8,128)(2,1)}, u32[]{:S(2)}) copy-start(bf16[1024,1024]{1,0:T(8,128)(2,1)} %all-gather.22.cloned.1.call-done) | copy-start | bytes 6291460
  457.5 77.1 %copy-start.18 = (bf16[2,272,1024]{2,1,0:T(8,128)(2,1)S(1)}, bf16[2,272,1024]{2,1,0:T(8,128)(2,1)}, u32[]{:S(2)}) copy-start(bf16[2,272,1024]{2,1,0:T(8,128)(2,1)} %param.23) | copy-start | bytes 3342340
  457.5 77.1 %copy-start.92 = (f32[1,1024]{1,0:T(1,128)S(1)}, f32[1,1024]{1,0:T(1,128)}, u32[]{:S(2)}) copy-start(f32[1,1024]{1,0:T(1,128)} %get-tuple-element.127) | copy-start | bytes 12292
  457.5 130.5 %all-gather.28.cloned.1.call-start = ((), (), s32[]{:S(2)}) async-start(), calls=%async_computation.27 | async-start | bytes 2785280 | tf_op jit(solution)/shard_map/all_gather | solution.py:234
  540.1 96.6 %all-gather.32.cloned.1.call-start = ((), (), s32[]{:S(2)}) async-start(), calls=%async_computation.31 | async-start | bytes 2785280 | tf_op jit(solution)/shard_map/all_gather | solution.py:234
  540.9 142.9 %reduce-scatter.33.cloned.1.call-start = ((), (), s32[]{:S(2)}) async-start(), calls=%async_computation.28 | async-start | bytes 2785280 | tf_op jit(solution)/shard_map/reduce_scatter | solution.py:244
  588.0 10.7 copy-start.159
  602.7 128.7 %reduce-scatter.37.cloned.1.call-start = ((), (), s32[]{:S(2)}) async-start(), calls=%async_computation.32 | async-start | bytes 2785280 | tf_op jit(solution)/shard_map/reduce_scatter | solution.py:244
  647.5 83.9 %copy-start.146 = (f32[1,1024]{1,0:T(1,128)S(1)}, f32[1,1024]{1,0:T(1,128)}, u32[]{:S(2)}) copy-start(f32[1,1024]{1,0:T(1,128)} %get-tuple-element.131) | copy-start | bytes 12292
  651.4 138.3 %all-gather.30.cloned.1.call-start = ((), (), s32[]{:S(2)}) async-start(), calls=%async_computation.29 | async-start | bytes 2785280 | tf_op jit(solution)/shard_map/all_gather | solution.py:255
  739.4 50.3 %copy-start.38 = (bf16[256,1024]{1,0:T(8,128)(2,1)S(1)}, bf16[256,1024]{1,0:T(8,128)(2,1)}, u32[]{:S(2)}) copy-start(bf16[256,1024]{1,0:T(8,128)(2,1)} %all_gather.75) | copy-start | bytes 1572868
  741.8 96.5 %all-gather.34.cloned.1.call-start = ((), (), s32[]{:S(2)}) async-start(), calls=%async_computation.33 | async-start | bytes 2785280 | tf_op jit(solution)/shard_map/all_gather | solution.py:255
  742.7 194.0 %reduce-scatter.35.cloned.1.call-start = ((), (), s32[]{:S(2)}) async-start(), calls=%async_computation.30 | async-start | bytes 2785280 | tf_op jit(solution)/shard_map/reduce_scatter | solution.py:297
  742.8 49.6 %copy-start.23 = (bf16[1088,256]{0,1:T(8,128)(2,1)S(1)}, bf16[1088,256]{0,1:T(8,128)(2,1)}, u32[]{:S(2)}) copy-start(bf16[1088,256]{0,1:T(8,128)(2,1)} %copy-done.22) | copy-start | bytes 1671172
  862.0 15.6 %copy-start.46 = (bf16[4,64,1088]{2,1,0:T(8,128)(2,1)}, bf16[4,64,1088]{2,1,0:T(8,128)(2,1)S(1)}, u32[]{:S(2)}) copy-start(bf16[4,64,1088]{2,1,0:T(8,128)(2,1)S(1)} %get-tuple-element.188) | copy-start | bytes 1671172
  879.9 92.7 %reduce-scatter.39.cloned.1.call-start = ((), (), s32[]{:S(2)}) async-start(), calls=%async_computation.34 | async-start | bytes 2785280 | tf_op jit(solution)/shard_map/reduce_scatter | solution.py:297
  922.8 108.0 %reduce-scatter.55.cloned.1.call-start = ((), (), s32[]{:S(2)}) async-start(), calls=%async_computation.42 | async-start | bytes 589824
  932.7 39.9 %copy-start.13 = (bf16[2,272,1024]{2,1,0:T(8,128)(2,1)S(1)}, bf16[2,272,1024]{2,1,0:T(8,128)(2,1)}, u32[]{:S(2)}) copy-start(bf16[2,272,1024]{2,1,0:T(8,128)(2,1)} %param.12) | copy-start | bytes 3342340
  932.7 39.9 %copy-start.90 = (f32[1,1024]{1,0:T(1,128)S(1)}, f32[1,1024]{1,0:T(1,128)}, u32[]{:S(2)}) copy-start(f32[1,1024]{1,0:T(1,128)} %copy-done.89) | copy-start | bytes 12292
  932.7 39.9 %copy-start.107 = (f32[272]{0:T(512)S(1)}, f32[272]{0:T(512)}, u32[]{:S(2)}) copy-start(f32[272]{0:T(512)} %copy-done.106) | copy-start | bytes 3268
  932.7 39.9 %copy-start.109 = (f32[272]{0:T(512)S(1)}, f32[272]{0:T(512)}, u32[]{:S(2)}) copy-start(f32[272]{0:T(512)} %copy-done.108) | copy-start | bytes 3268
  932.7 39.9 %copy-start.112 = (f32[272]{0:T(512)S(1)}, f32[272]{0:T(512)}, u32[]{:S(2)}) copy-start(f32[272]{0:T(512)} %copy-done.111) | copy-start | bytes 3268
  932.7 39.9 %copy-start.114 = (f32[272]{0:T(512)S(1)}, f32[272]{0:T(512)}, u32[]{:S(2)}) copy-start(f32[272]{0:T(512)} %copy-done.113) | copy-start | bytes 3268
  932.7 113.7 %reduce-scatter.49.cloned.1.call-start = ((), (), s32[]{:S(2)}) async-start(), calls=%async_computation.39 | async-start | bytes 147456
  933.6 41.4 %copy-start.131 = (f32[1024]{0:T(1024)S(1)}, f32[1024]{0:T(1024)}, u32[]{:S(2)}) copy-start(f32[1024]{0:T(1024)} %get-tuple-element.17) | copy-start | bytes 12292
  933.6 41.4 %copy-start.132 = (f32[1024]{0:T(1024)S(1)}, f32[1024]{0:T(1024)}, u32[]{:S(2)}) copy-start(f32[1024]{0:T(1024)} %get-tuple-element.28) | copy-start | bytes 12292
  933.6 41.4 %copy-start.135 = (f32[1024]{0:T(1024)S(1)}, f32[1024]{0:T(1024)}, u32[]{:S(2)}) copy-start(f32[1024]{0:T(1024)} %get-tuple-element.15) | copy-start | bytes 12292
  933.6 41.4 %copy-start.136 = (f32[1024]{0:T(1024)S(1)}, f32[1024]{0:T(1024)}, u32[]{:S(2)}) copy-start(f32[1024]{0:T(1024)} %get-tuple-element.64) | copy-start | bytes 12292
  933.7 41.4 %copy-start.142 = (f32[1024]{0:T(1024)S(1)}, f32[1024]{0:T(1024)}, u32[]{:S(2)}) copy-start(f32[1024]{0:T(1024)} %get-tuple-element.25) | copy-start | bytes 12292
  933.7 41.4 %copy-start.143 = (f32[1024]{0:T(1024)S(1)}, f32[1024]{0:T(1024)}, u32[]{:S(2)}) copy-start(f32[1024]{0:T(1024)} %get-tuple-element.124) | copy-start | bytes 12292
  935.1 41.2 %copy-start.133 = (f32[1024]{0:T(1024)S(1)}, f32[1024]{0:T(1024)}, u32[]{:S(2)}) copy-start(f32[1024]{0:T(1024)} %get-tuple-element.38) | copy-start | bytes 12292
  935.1 41.2 %copy-start.134 = (f32[1024]{0:T(1024)S(1)}, f32[1024]{0:T(1024)}, u32[]{:S(2)}) copy-start(f32[1024]{0:T(1024)} %get-tuple-element.61) | copy-start | bytes 12292
  935.1 41.2 %copy-start.140 = (f32[1024]{0:T(1024)S(1)}, f32[1024]{0:T(1024)}, u32[]{:S(2)}) copy-start(f32[1024]{0:T(1024)} %get-tuple-element.50) | copy-start | bytes 12292
  935.1 41.2 %copy-start.141 = (f32[1024]{0:T(1024)S(1)}, f32[1024]{0:T(1024)}, u32[]{:S(2)}) copy-start(f32[1024]{0:T(1024)} %get-tuple-element.121) | copy-start | bytes 12292
  936.6 147.0 %reduce-scatter.51.cloned.1.call-start = ((), (), s32[]{:S(2)}) async-start(), calls=%async_computation.40 | async-start | bytes 589824
  976.2 145.0 %reduce-scatter.53.cloned.1.call-start = ((), (), s32[]{:S(2)}) async-start(), calls=%async_computation.41 | async-start | bytes 589824
  977.4 198.9 %reduce-scatter.47.cloned.1.call-start = ((), (), s32[]{:S(2)}) async-start(), calls=%async_computation.38 | async-start | bytes 4718592 | tf_op jit(solution)/shard_map/reduce_scatter | solution.py:322
  985.9 246.1 %reduce-scatter.45.cloned.1.call-start = ((), (), s32[]{:S(2)}) async-start(), calls=%async_computation.37 | async-start | bytes 4718592 | tf_op jit(solution)/shard_map/reduce_scatter | solution.py:320
  996.1 275.6 %reduce-scatter.43.cloned.1.call-start = ((), (), s32[]{:S(2)}) async-start(), calls=%async_computation.36 | async-start | bytes 1179648 | tf_op jit(solution)/shard_map/reduce_scatter | solution.py:319
  1001.6 320.1 %reduce-scatter.41.cloned.1.call-start = ((), (), s32[]{:S(2)}) async-start(), calls=%async_computation.35 | async-start | bytes 3538944 | tf_op jit(solution)/shard_map/reduce_scatter | solution.py:317
  1012.4 35.4 %copy-start.29 = (f32[272,1024]{1,0:T(8,128)S(1)}, f32[272,1024]{1,0:T(8,128)}, u32[]{:S(2)}) copy-start(f32[272,1024]{1,0:T(8,128)} %copy-done.28) | copy-start | bytes 3342340
  1012.4 35.4 %copy-start.31 = (f32[272,1024]{1,0:T(8,128)S(1)}, f32[272,1024]{1,0:T(8,128)}, u32[]{:S(2)}) copy-start(f32[272,1024]{1,0:T(8,128)} %copy-done.30) | copy-start | bytes 3342340
  (154 other events, 523.9 us)
Sparse Core Ops, SparseCore 0:
  9.9 28.3 all-gather.15
  40.5 48.3 all-gather.23
  91.0 47.1 all-gather.13
  186.1 44.8 reduce-scatter.24
  233.1 45.4 reduce-scatter.28
  280.3 27.2 all-gather.19
  309.8 48.3 all-gather.17
  360.0 26.7 all-gather.21
  388.4 48.3 all-gather.25
  438.9 44.8 reduce-scatter.26
  486.1 45.4 reduce-scatter.30
  540.3 47.7 all-gather.27
  589.6 47.1 all-gather.31
  638.9 44.8 reduce-scatter.32
  686.0 45.4 reduce-scatter.36
  741.9 47.7 all-gather.29
  791.1 47.1 all-gather.33
  880.0 44.8 reduce-scatter.34
  927.2 45.4 reduce-scatter.38
  976.1 33.5 reduce-scatter.54
  1013.0 33.3 reduce-scatter.48
  1049.5 34.1 reduce-scatter.50
  1087.0 34.1 reduce-scatter.52
  1125.0 51.3 reduce-scatter.46
  1180.6 51.3 reduce-scatter.44
  1235.6 36.0 reduce-scatter.42
  1275.5 46.1 reduce-scatter.40
where the time goes:
time: 1330 us
  waiting for transfers between devices  873 us (66%)
  matrix products  222 us (17%)
  blocking collectives  81.3 us (6%)
  other arithmetic  69 us (5%)
  local copies, waits for them, and re-layouts  62.5 us (5%)
  between operations  18.1 us (1%)
    all_gather x2, waiting for transfers between devices, on_device(): hidden_two = lax.all_gather(normed_two, 'mp', axis=0, tiled=True)  94 us
    unnamed x31, waiting for transfers between devices  87.3 us
    all_gather x2, waiting for transfers between devices, on_device(): grad_branch_all = lax.all_gather(grad_branch, 'mp', axis=0, tiled=True)  82.7 us
    all_gather x2, waiting for transfers between devices, on_device(): grad_f_all = lax.all_gather(grad_f, 'mp', axis=0, tiled=True)  80.7 us
    reduce_scatter x2, waiting for transfers between devices, on_device(): lax.psum_scatter(ffn_back(jnp.int32(0), lax.axis_size('mp') * share).asty...  79.8 us
    reduce_scatter x2, waiting for transfers between devices, on_device(): lax.psum_scatter(ffn_term(jnp.int32(0), lax.axis_size('mp') * share).asty...  72.7 us
    all_gather x2, waiting for transfers between devices, on_device(): hidden_in = lax.all_gather(normed, 'mp', axis=0, tiled=True)  67.9 us
    reduce_scatter x2, waiting for transfers between devices, on_device(): lax.psum_scatter(out_term(jnp.int32(0), lax.axis_size('mp') * share).asty...  59.8 us
  transfers between devices with their start and end apart: 27, of which 24 were waited for; matrix products, arithmetic and copies ran while one was open for 17% of the time, Pallas kernels for 0%

commit v1 on v0

--- a/solution.py
+++ b/solution.py
@@ -1,3 +1,4 @@
+import functools
 import math
 import jax
 import jax.numpy as jnp
@@ -7,6 +8,24 @@
 HEAD_DIM = 64
 ALPHA = 32.0
 EPS = 1e-05
+
+
+def put_frame(target, which_axis):
+    k_all = lax.axis_size(which_axis)
+    frame_out = target
+    tile_out = [(nth - 1, nth) for nth in range(1, k_all)] + [(k_all - 1, 0)]
+    buffers = [frame_out]
+    u = 0
+    while u < k_all - 1:
+        frame_out = lax.ppermute(frame_out, axis_name=which_axis, perm=tile_out)
+        buffers += [frame_out]
+        u = u + 1
+    odd = jnp.concatenate([*reversed(buffers)], axis=0)
+    moved = lax.axis_index(which_axis)
+    return jnp.roll(odd, shift=(moved + 1) * frame_out.shape[0], axis=0)
+
+
+view_floor = functools.partial(put_frame, which_axis="mp")
 
 
 def normalize(value, gain, shift):
@@ -167,7 +186,7 @@
         )
         middle = x_rows + normalize(branch, gains[1], shifts[1])
         normed_two = normalize(middle, gains[2], shifts[2]).astype(jnp.bfloat16)
-        hidden_two = lax.all_gather(normed_two, "mp", axis=0, tiled=True)
+        hidden_two = view_floor(normed_two)
         pre = jnp.dot(hidden_two, w_up, preferred_element_type=jnp.float32) + b_up.astype(
             jnp.float32
         )

time: 1330 us -> 1280 us (0.962)
  waiting for transfers between devices: 873 us -> 793 us
  other arithmetic: 69 us -> 101 us
    all_gather x2 -> x0, waiting for transfers between devices: 94 us -> none  [on_device(): hidden_two = lax.all_gather(normed_two, 'mp', axis=0, tiled=True)]
    ppermute x0 -> x6, waiting for transfers between devices: none -> 54 us  [put_frame(): frame_out = lax.ppermute(frame_out, axis_name=which_axis, perm=tile_out)]
    concatenate x0 -> x2, other arithmetic: none -> 21.6 us  [put_frame(): return jnp.roll(odd, shift=(moved + 1) * frame_out.shape[0], axis=0)]
    unnamed x31 -> x29, waiting for transfers between devices: 87.3 us -> 86 us
    unnamed x392 -> x402, local copies, waits for them, and re-layouts: 28.4 us -> 28.4 us
  transfers between devices with their start and end apart: 27 -> 31, of which waited for: 24 -> 25; matrix products, arithmetic and copies ran while one was open for 17% -> 20% of each run, Pallas kernels for 0% -> 0%
where the time goes in v1:
time: 1280 us; the launch traced here: 1270 us
  waiting for transfers between devices  793 us (62%)
  matrix products  211 us (16%)
  other arithmetic  101 us (8%)
  blocking collectives  81.3 us (6%)
  local copies, waits for them, and re-layouts  62.8 us (5%)
  between operations  17.8 us (1%)
    unnamed x29, waiting for transfers between devices  86 us
    all_gather x2, waiting for transfers between devices, on_device(): grad_branch_all = lax.all_gather(grad_branch, 'mp', axis=0, tiled=True)  82.4 us
    all_gather x2, waiting for transfers between devices, on_device(): grad_f_all = lax.all_gather(grad_f, 'mp', axis=0, tiled=True)  79.8 us
    reduce_scatter x2, waiting for transfers between devices, on_device(): lax.psum_scatter(ffn_back(jnp.int32(0), lax.axis_size('mp') * share).asty...  78.9 us
    all_gather x2, waiting for transfers between devices, on_device(): hidden_in = lax.all_gather(normed, 'mp', axis=0, tiled=True)  67.8 us
    reduce_scatter x2, waiting for transfers between devices, on_device(): lax.psum_scatter(ffn_term(jnp.int32(0), lax.axis_size('mp') * share).asty...  61.1 us
    reduce_scatter x2, waiting for transfers between devices, on_device(): lax.psum_scatter(out_term(jnp.int32(0), lax.axis_size('mp') * share).asty...  59.9 us
    reduce_scatter x1, waiting for transfers between devices, on_device(): lax.psum_scatter(local[3], 'dp', scatter_dimension=0, tiled=True)  55.7 us
  transfers between devices with their start and end apart: 31, of which 25 were waited for; matrix products, arithmetic and copies ran while one was open for 20% of the time, Pallas kernels for 0%

profile of v1, /device:TPU:0, one launch (start us, length us, event | category | flops | bytes accessed | tf_op | source)
XLA Modules:
  0.0 1272.0 jit_solution(6362943127267193362)
XLA Ops:
  8.0 10.5 all_gather.30
  18.4 8.7 all_gather.31
  34.5 7.9 all-gather
  42.7 10.7 all_gather.69
  53.9 3.5 fusion.126
  57.4 31.5 %all-gather.20.cloned.1.call-done = bf16[1088,1024]{1,0:T(8,128)(2,1)} async-done(((bf16[272,1024]{1,0:T(8,128)(2,1)}), bf16[1088,1024]{1,0:T(8,128)(2,1)}) %all-gather.20.cloned.1.call-update) | async-done | bytes 2228240 | tf_op jit(solution)/shard_map/all_gather | solution.py:160
  88.9 3.3 convolution_convert_fusion.8
  101.9 36.3 %all-gather.12.cloned.1.call-done = bf16[1088,1024]{1,0:T(8,128)(2,1)} async-done(((bf16[272,1024]{1,0:T(8,128)(2,1)}), bf16[1088,1024]{1,0:T(8,128)(2,1)}) %all-gather.12.cloned.1.call-update) | async-done | bytes 2228240 | tf_op jit(solution)/shard_map/all_gather | solution.py:160
  146.4 3.2 fusion.37
  151.0 2.7 fusion.36
  154.0 3.5 convolution_convert_fusion.9
  168.9 2.6 fusion.145
  208.7 9.0 all_gather.70
  217.7 13.6 %reduce-scatter.25.cloned.1.call-done = bf16[272,1024]{1,0:T(8,128)(2,1)} async-done(((bf16[1088,1024]{1,0:T(8,128)(2,1)}), bf16[272,1024]{1,0:T(8,128)(2,1)}) %reduce-scatter.25.cloned.1.call-update) | async-done | bytes 557072 | tf_op jit(solution)/shard_map/reduce_scatter | solution.py:179
  232.5 46.3 %reduce-scatter.29.cloned.1.call-done = bf16[272,1024]{1,0:T(8,128)(2,1)} async-done(((bf16[1088,1024]{1,0:T(8,128)(2,1)}), bf16[272,1024]{1,0:T(8,128)(2,1)}) %reduce-scatter.29.cloned.1.call-update) | async-done | bytes 557072 | tf_op jit(solution)/shard_map/reduce_scatter | solution.py:179
  287.5 15.0 %collective-permute-done = bf16[272,1024]{1,0:T(8,128)(2,1)S(1)} collective-permute-done((bf16[272,1024]{1,0:T(8,128)(2,1)S(1)}, bf16[272,1024]{1,0:T(8,128)(2,1)S(1)}, u32[]{:S(2)}, u32[]{:S(2)}) %collective-permute-start) | collective-permute-done | bytes 557088 | tf_op jit(solution)/shard_map/ppermute | solution.py:20
  302.5 12.0 collective-permute-done.3
  314.5 11.9 collective-permute-done.1
  326.5 8.7 all-gather.1
  335.2 3.1 collective-permute-done.4
  338.4 11.9 collective-permute-done.2
  350.3 11.3 fusion.84
  361.6 15.7 %multiply_convert_fusion.9 = (bf16[1088,1024]{1,0:T(8,128)(2,1)}, f32[1088,1024]{1,0:T(8,128)}, f32[1088,1024]{1,0:T(8,128)}) fusion(f32[1024]{0:T(1024)S(1)} %bitcast.598, bf16[1088,1024]{1,0:T(8,128)(2,1)} %fusion.84, bf16[1024,1024]{1,0:T(8,128)(2,1)} %all-gather.16.cloned.1.call-done), kind=kOutput, calls=%fused_computation.93 | convolution fusion | flops 2355232768 | bytes 15470592 | tf_op jit(solution)/shard_map/dot_general | solution.py:190
  377.2 6.1 convolution_convert_fusion.4
  383.9 10.3 fusion.77
  394.2 13.3 %multiply_convert_fusion.8 = (bf16[1088,1024]{1,0:T(8,128)(2,1)S(1)}, f32[1088,1024]{1,0:T(8,128)}, f32[1088,1024]{1,0:T(8,128)}) fusion(f32[1024]{0:T(1024)S(1)} %bitcast.599, bf16[1088,1024]{1,0:T(8,128)(2,1)S(1)} %fusion.77, bf16[1024,1024]{1,0:T(8,128)(2,1)S(1)} %copy-done.166), kind=kOutput, calls=%fused_computation.80 | convolution fusion | flops 2355232768 | bytes 15470592 | tf_op jit(solution)/shard_map/dot_general | solution.py:190
  408.9 3.9 convolution_convert_fusion.2
  413.1 14.6 %reduce-scatter.27.cloned.1.call-done = bf16[272,1024]{1,0:T(8,128)(2,1)} async-done(((bf16[1088,1024]{1,0:T(8,128)(2,1)}), bf16[272,1024]{1,0:T(8,128)(2,1)}) %reduce-scatter.27.cloned.1.call-update) | async-done | bytes 557072 | tf_op jit(solution)/shard_map/reduce_scatter | solution.py:199
  429.0 46.5 %reduce-scatter.31.cloned.1.call-done = bf16[272,1024]{1,0:T(8,128)(2,1)} async-done(((bf16[1088,1024]{1,0:T(8,128)(2,1)}), bf16[272,1024]{1,0:T(8,128)(2,1)}) %reduce-scatter.31.cloned.1.call-update) | async-done | bytes 557072 | tf_op jit(solution)/shard_map/reduce_scatter | solution.py:199
  478.6 3.0 fusion.168
  484.9 47.1 %all-gather.26.cloned.1.call-done = bf16[1088,1024]{1,0:T(8,128)(2,1)} async-done(((bf16[272,1024]{1,0:T(8,128)(2,1)}), bf16[1088,1024]{1,0:T(8,128)(2,1)}) %all-gather.26.cloned.1.call-update) | async-done | bytes 2228240 | tf_op jit(solution)/shard_map/all_gather | solution.py:253
  532.0 4.8 fusion.244
  536.8 5.7 convert_reduce_fusion
  543.9 3.9 convolution_convert_fusion
  548.0 32.7 %all-gather.22.cloned.1.call-done = bf16[1088,1024]{1,0:T(8,128)(2,1)} async-done(((bf16[272,1024]{1,0:T(8,128)(2,1)}), bf16[1088,1024]{1,0:T(8,128)(2,1)}) %all-gather.22.cloned.1.call-update) | async-done | bytes 2228240 | tf_op jit(solution)/shard_map/all_gather | solution.py:253
  580.8 4.8 fusion.242
  585.6 5.8 convert_reduce_fusion.1
  592.7 3.9 convolution_convert_fusion.1
  596.6 31.1 %reduce-scatter.37.cloned.1.call-done = bf16[272,1024]{1,0:T(8,128)(2,1)} async-done(((bf16[1088,1024]{1,0:T(8,128)(2,1)}), bf16[272,1024]{1,0:T(8,128)(2,1)}) %reduce-scatter.37.cloned.1.call-update) | async-done | bytes 557072 | tf_op jit(solution)/shard_map/reduce_scatter | solution.py:263
  627.8 47.8 %reduce-scatter.33.cloned.1.call-done = bf16[272,1024]{1,0:T(8,128)(2,1)} async-done(((bf16[1088,1024]{1,0:T(8,128)(2,1)}), bf16[272,1024]{1,0:T(8,128)(2,1)}) %reduce-scatter.33.cloned.1.call-update) | async-done | bytes 557072 | tf_op jit(solution)/shard_map/reduce_scatter | solution.py:263
  675.6 5.0 fusion.182
  680.6 2.7 multiply_reduce_fusion.9
  686.9 46.9 %all-gather.24.cloned.1.call-done = bf16[1088,1024]{1,0:T(8,128)(2,1)} async-done(((bf16[272,1024]{1,0:T(8,128)(2,1)}), bf16[1088,1024]{1,0:T(8,128)(2,1)}) %all-gather.24.cloned.1.call-update) | async-done | bytes 2228240 | tf_op jit(solution)/shard_map/all_gather | solution.py:274
  736.5 4.1 multiply_reduce_fusion.7
  746.9 35.5 %all-gather.28.cloned.1.call-done = bf16[1088,1024]{1,0:T(8,128)(2,1)} async-done(((bf16[272,1024]{1,0:T(8,128)(2,1)}), bf16[1088,1024]{1,0:T(8,128)(2,1)}) %all-gather.28.cloned.1.call-update) | async-done | bytes 2228240 | tf_op jit(solution)/shard_map/all_gather | solution.py:274
  792.1 4.1 multiply_reduce_fusion.6
  796.2 3.5 convolution_add_fusion.18
  825.0 4.3 multiply_reduce_fusion
  868.4 7.3 fusion.248
  880.7 35.8 %reduce-scatter.39.cloned.1.call-done = bf16[272,1024]{1,0:T(8,128)(2,1)} async-done(((bf16[1088,1024]{1,0:T(8,128)(2,1)}), bf16[272,1024]{1,0:T(8,128)(2,1)}) %reduce-scatter.39.cloned.1.call-update) | async-done | bytes 557072 | tf_op jit(solution)/shard_map/reduce_scatter | solution.py:316
  921.4 8.5 convolution_add_fusion.22
  929.9 5.5 fusion.247
  935.4 4.5 convolution_add_fusion.23
  941.0 2.6 fusion.246
  945.8 2.7 convolution_bitcast_fusion
  958.2 13.5 %all-reduce = f32[1024]{0:T(1024)S(1)} all-reduce(f32[1024]{0:T(1024)S(1)} %add.589), channel_id=23, replica_groups=mesh['dp'=8,'mp'=4] {'dp'}, use_global_device_ids=true, to_apply=%region_77.79.clone | all-reduce | flops 1024 | bytes 8192
  975.4 14.3 %reduce-scatter.49.cloned.1.call-done = f32[32,2]{1,0:T(8,128)} async-done(((f32[256,2]{1,0:T(8,128)}), f32[32,2]{1,0:T(8,128)}) %reduce-scatter.49.cloned.1.call-update) | async-done | bytes 272
  994.8 32.1 %reduce-scatter.51.cloned.1.call-done = f32[128,4]{1,0:T(8,128)} async-done(((f32[1024,4]{1,0:T(8,128)}), f32[128,4]{1,0:T(8,128)}) %reduce-scatter.51.cloned.1.call-update) | async-done | bytes 2064
  1027.8 36.7 %reduce-scatter.53.cloned.1.call-done = f32[128,4]{1,0:T(8,128)} async-done(((f32[1024,4]{1,0:T(8,128)}), f32[128,4]{1,0:T(8,128)}) %reduce-scatter.53.cloned.1.call-update) | async-done | bytes 2064
  1065.3 12.4 all-reduce.1
  1077.7 42.0 %reduce-scatter.47.cloned.1.call-done = f32[128,1024]{1,0:T(8,128)} async-done(((f32[1024,1024]{1,0:T(8,128)}), f32[128,1024]{1,0:T(8,128)}) %reduce-scatter.47.cloned.1.call-update) | async-done | bytes 524304 | tf_op jit(solution)/shard_map/reduce_scatter | solution.py:341
  1119.7 55.7 %reduce-scatter.45.cloned.1.call-done = f32[128,1024]{1,0:T(8,128)} async-done(((f32[1024,1024]{1,0:T(8,128)}), f32[128,1024]{1,0:T(8,128)}) %reduce-scatter.45.cloned.1.call-update) | async-done | bytes 524304 | tf_op jit(solution)/shard_map/reduce_scatter | solution.py:339
  1175.4 39.7 %reduce-scatter.43.cloned.1.call-done = f32[32,1024]{1,0:T(8,128)} async-done(((f32[256,1024]{1,0:T(8,128)}), f32[32,1024]{1,0:T(8,128)}) %reduce-scatter.43.cloned.1.call-update) | async-done | bytes 131088 | tf_op jit(solution)/shard_map/reduce_scatter | solution.py:338
  1215.0 50.2 %reduce-scatter.41.cloned.1.call-done = f32[3,128,256]{2,1,0:T(8,128)} async-done(((f32[3,1024,256]{2,1,0:T(8,128)}), f32[3,128,256]{2,1,0:T(8,128)}) %reduce-scatter.41.cloned.1.call-update) | async-done | bytes 393232 | tf_op jit(solution)/shard_map/reduce_scatter | solution.py:336
  (667 shorter events, 216.6 us)
Async XLA Ops:
  7.2 25.0 %copy-start.12 = (bf16[2,272,1024]{2,1,0:T(8,128)(2,1)S(1)}, bf16[2,272,1024]{2,1,0:T(8,128)(2,1)}, u32[]{:S(2)}) copy-start(bf16[2,272,1024]{2,1,0:T(8,128)(2,1)} %param.14) | copy-start | bytes 3342340
  7.2 50.2 %all-gather.14.cloned.1.call-start = ((), (), s32[]{:S(2)}) async-start(), calls=%async_computation.17 | async-start | bytes 1769472 | tf_op jit(solution)/shard_map/all_gather | solution.py:133
  7.9 81.0 %all-gather.20.cloned.1.call-start = ((), (), s32[]{:S(2)}) async-start(), calls=%async_computation.22 | async-start | bytes 2785280 | tf_op jit(solution)/shard_map/all_gather | solution.py:160
  33.7 104.5 %all-gather.12.cloned.1.call-start = ((), (), s32[]{:S(2)}) async-start(), calls=%async_computation.16 | async-start | bytes 2785280 | tf_op jit(solution)/shard_map/all_gather | solution.py:160
  34.4 196.8 %reduce-scatter.25.cloned.1.call-start = ((), (), s32[]{:S(2)}) async-start(), calls=%async_computation.18 | async-start | bytes 2785280 | tf_op jit(solution)/shard_map/reduce_scatter | solution.py:179
  53.9 39.6 %copy-start.160 = (f32[1,256]{1,0:T(1,128)}, f32[1,256]{1,0:T(1,128)S(1)}, u32[]{:S(2)}) copy-start(f32[1,256]{1,0:T(1,128)S(1)} %get-tuple-element.152) | copy-start | bytes 3076
  57.4 36.1 %copy-start.32 = (bf16[3,1024,256]{2,1,0:T(8,128)(2,1)S(1)}, bf16[3,1024,256]{2,1,0:T(8,128)(2,1)}, u32[]{:S(2)}) copy-start(bf16[3,1024,256]{2,1,0:T(8,128)(2,1)} %all-gather.14.cloned.1.call-done) | copy-start | bytes 4718596
  93.5 101.7 %copy-start.8 = (bf16[1088,256]{0,1:T(8,128)(2,1)}, bf16[1088,256]{0,1:T(8,128)(2,1)S(1)}, u32[]{:S(2)}) copy-start(bf16[1088,256]{0,1:T(8,128)(2,1)S(1)} %copy.138) | copy-start | bytes 1671172
  151.0 51.4 %copy-start.20 = (bf16[1088,256]{0,1:T(8,128)(2,1)}, bf16[1088,256]{0,1:T(8,128)(2,1)S(1)}, u32[]{:S(2)}) copy-start(bf16[1088,256]{0,1:T(8,128)(2,1)S(1)} %copy.136) | copy-start | bytes 1671172
  154.0 25.4 %copy-start.22 = (bf16[1088,256]{0,1:T(8,128)(2,1)}, bf16[1088,256]{0,1:T(8,128)(2,1)S(1)}, u32[]{:S(2)}) copy-start(bf16[1088,256]{0,1:T(8,128)(2,1)S(1)} %copy.130) | copy-start | bytes 1671172
  158.8 18.3 %copy-start.10 = (bf16[1088,256]{0,1:T(8,128)(2,1)}, bf16[1088,256]{0,1:T(8,128)(2,1)S(1)}, u32[]{:S(2)}) copy-start(bf16[1088,256]{0,1:T(8,128)(2,1)S(1)} %copy.132) | copy-start | bytes 1671172
  186.3 92.6 %reduce-scatter.29.cloned.1.call-start = ((), (), s32[]{:S(2)}) async-start(), calls=%async_computation.23 | async-start | bytes 2785280 | tf_op jit(solution)/shard_map/reduce_scatter | solution.py:179
  208.0 73.9 %copy-start.99 = (f32[1,1024]{1,0:T(1,128)S(1)}, f32[1,1024]{1,0:T(1,128)}, u32[]{:S(2)}) copy-start(f32[1,1024]{1,0:T(1,128)} %get-tuple-element.130) | copy-start | bytes 12292
  208.0 73.9 %copy-start.157 = (f32[1,1024]{1,0:T(1,128)S(1)}, f32[1,1024]{1,0:T(1,128)}, u32[]{:S(2)}) copy-start(f32[1,1024]{1,0:T(1,128)} %get-tuple-element.134) | copy-start | bytes 12292
  208.1 153.5 %all-gather.16.cloned.1.call-start = ((), (), s32[]{:S(2)}) async-start(), calls=%async_computation.19 | async-start | bytes 2359296 | tf_op jit(solution)/shard_map/all_gather | solution.py:136
  208.7 168.6 %all-gather.18.cloned.1.call-start = ((), (), s32[]{:S(2)}) async-start(), calls=%async_computation.20 | async-start | bytes 2359296 | tf_op jit(solution)/shard_map/all_gather | solution.py:138
  284.3 42.2 %copy-start.163 = (bf16[128]{0:T(256)(128)(2,1)S(1)}, bf16[128]{0:T(256)(128)(2,1)}, u32[]{:S(2)}) copy-start(bf16[128]{0:T(256)(128)(2,1)} %param.20) | copy-start | bytes 772
  285.1 17.4 %collective-permute-start = (bf16[272,1024]{1,0:T(8,128)(2,1)S(1)}, bf16[272,1024]{1,0:T(8,128)(2,1)S(1)}, u32[]{:S(2)}, u32[]{:S(2)}) collective-permute-start(bf16[272,1024]{1,0:T(8,128)(2,1)S(1)} %get-tuple-element.136), channel_id=1, source_target_pairs={{0,1},{1,2},{2,3},{3,0},{4,5},{5,6},{6,7},{7,4},{8,9},{9,10},{10,1... | collective-permute-start | bytes 1671176 | tf_op jit(solution)/shard_map/ppermute | solution.py:20
  285.1 29.4 %collective-permute-start.3 = (bf16[272,1024]{1,0:T(8,128)(2,1)S(1)}, bf16[272,1024]{1,0:T(8,128)(2,1)}, u32[]{:S(2)}, u32[]{:S(2)}) collective-permute-start(bf16[272,1024]{1,0:T(8,128)(2,1)S(1)} %get-tuple-element.137), channel_id=1, source_target_pairs={{0,1},{1,2},{2,3},{3,0},{4,5},{5,6},{6,7},{7,4},{8,9},{9,10},{10,1... | collective-permute-start | bytes 1671176 | tf_op jit(solution)/shard_map/ppermute | solution.py:20
  302.5 24.0 %collective-permute-start.1 = (bf16[272,1024]{1,0:T(8,128)(2,1)S(1)}, bf16[272,1024]{1,0:T(8,128)(2,1)}, u32[]{:S(2)}, u32[]{:S(2)}) collective-permute-start(bf16[272,1024]{1,0:T(8,128)(2,1)S(1)} %collective-permute-done), channel_id=1, source_target_pairs={{0,1},{1,2},{2,3},{3,0},{4,5},{5,6},{6,7},{7,4},{8,9},{9,10},{10,1... | collective-permute-start | bytes 1671176 | tf_op jit(solution)/shard_map/ppermute | solution.py:20
  314.5 23.9 %collective-permute-start.4 = (bf16[272,1024]{1,0:T(8,128)(2,1)}, bf16[272,1024]{1,0:T(8,128)(2,1)}, u32[]{:S(2)}, u32[]{:S(2)}) collective-permute-start(bf16[272,1024]{1,0:T(8,128)(2,1)} %collective-permute-done.3), channel_id=1, source_target_pairs={{0,1},{1,2},{2,3},{3,0},{4,5},{5,6},{6,7},{7,4},{8,9},{9,10},{10,1... | collective-permute-start | bytes 1671176 | tf_op jit(solution)/shard_map/ppermute | solution.py:20
  326.4 23.9 %collective-permute-start.2 = (bf16[272,1024]{1,0:T(8,128)(2,1)}, bf16[272,1024]{1,0:T(8,128)(2,1)}, u32[]{:S(2)}, u32[]{:S(2)}) collective-permute-start(bf16[272,1024]{1,0:T(8,128)(2,1)} %collective-permute-done.1), channel_id=1, source_target_pairs={{0,1},{1,2},{2,3},{3,0},{4,5},{5,6},{6,7},{7,4},{8,9},{9,10},{10,1... | collective-permute-start | bytes 1671176 | tf_op jit(solution)/shard_map/ppermute | solution.py:20
  326.5 101.2 %reduce-scatter.27.cloned.1.call-start = ((), (), s32[]{:S(2)}) async-start(), calls=%async_computation.21 | async-start | bytes 2785280 | tf_op jit(solution)/shard_map/reduce_scatter | solution.py:199
  338.4 45.5 %collective-permute-start.5 = (bf16[272,1024]{1,0:T(8,128)(2,1)}, bf16[272,1024]{1,0:T(8,128)(2,1)}, u32[]{:S(2)}, u32[]{:S(2)}) collective-permute-start(bf16[272,1024]{1,0:T(8,128)(2,1)} %collective-permute-done.4), channel_id=1, source_target_pairs={{0,1},{1,2},{2,3},{3,0},{4,5},{5,6},{6,7},{7,4},{8,9},{9,10},{10,1... | collective-permute-start | bytes 1671176 | tf_op jit(solution)/shard_map/ppermute | solution.py:20
  383.4 92.1 %reduce-scatter.31.cloned.1.call-start = ((), (), s32[]{:S(2)}) async-start(), calls=%async_computation.24 | async-start | bytes 2785280 | tf_op jit(solution)/shard_map/reduce_scatter | solution.py:199
  412.8 65.8 %copy-start.18 = (bf16[2,272,1024]{2,1,0:T(8,128)(2,1)S(1)}, bf16[2,272,1024]{2,1,0:T(8,128)(2,1)}, u32[]{:S(2)}) copy-start(bf16[2,272,1024]{2,1,0:T(8,128)(2,1)} %param.25) | copy-start | bytes 3342340
  412.8 65.8 %copy-start.98 = (f32[1,1024]{1,0:T(1,128)S(1)}, f32[1,1024]{1,0:T(1,128)}, u32[]{:S(2)}) copy-start(f32[1,1024]{1,0:T(1,128)} %get-tuple-element.128) | copy-start | bytes 12292
  412.8 119.2 %all-gather.26.cloned.1.call-start = ((), (), s32[]{:S(2)}) async-start(), calls=%async_computation.29 | async-start | bytes 2785280 | tf_op jit(solution)/shard_map/all_gather | solution.py:253
  484.1 96.7 %all-gather.22.cloned.1.call-start = ((), (), s32[]{:S(2)}) async-start(), calls=%async_computation.25 | async-start | bytes 2785280 | tf_op jit(solution)/shard_map/all_gather | solution.py:253
  484.8 142.9 %reduce-scatter.37.cloned.1.call-start = ((), (), s32[]{:S(2)}) async-start(), calls=%async_computation.30 | async-start | bytes 2785280 | tf_op jit(solution)/shard_map/reduce_scatter | solution.py:263
  547.8 127.8 %reduce-scatter.33.cloned.1.call-start = ((), (), s32[]{:S(2)}) async-start(), calls=%async_computation.26 | async-start | bytes 2785280 | tf_op jit(solution)/shard_map/reduce_scatter | solution.py:263
  592.7 82.8 %copy-start.156 = (f32[1,1024]{1,0:T(1,128)S(1)}, f32[1,1024]{1,0:T(1,128)}, u32[]{:S(2)}) copy-start(f32[1,1024]{1,0:T(1,128)} %get-tuple-element.132) | copy-start | bytes 12292
  596.6 137.2 %all-gather.24.cloned.1.call-start = ((), (), s32[]{:S(2)}) async-start(), calls=%async_computation.27 | async-start | bytes 2785280 | tf_op jit(solution)/shard_map/all_gather | solution.py:274
  683.5 50.3 %copy-start.38 = (bf16[256,1024]{1,0:T(8,128)(2,1)S(1)}, bf16[256,1024]{1,0:T(8,128)(2,1)}, u32[]{:S(2)}) copy-start(bf16[256,1024]{1,0:T(8,128)(2,1)} %all_gather.69) | copy-start | bytes 1572868
  685.9 96.5 %all-gather.28.cloned.1.call-start = ((), (), s32[]{:S(2)}) async-start(), calls=%async_computation.31 | async-start | bytes 2785280 | tf_op jit(solution)/shard_map/all_gather | solution.py:274
  686.8 193.9 %reduce-scatter.35.cloned.1.call-start = ((), (), s32[]{:S(2)}) async-start(), calls=%async_computation.28 | async-start | bytes 2785280 | tf_op jit(solution)/shard_map/reduce_scatter | solution.py:316
  686.9 49.5 %copy-start.23 = (bf16[1088,256]{0,1:T(8,128)(2,1)S(1)}, bf16[1088,256]{0,1:T(8,128)(2,1)}, u32[]{:S(2)}) copy-start(bf16[1088,256]{0,1:T(8,128)(2,1)} %copy-done.22) | copy-start | bytes 1671172
  824.0 92.6 %reduce-scatter.39.cloned.1.call-start = ((), (), s32[]{:S(2)}) async-start(), calls=%async_computation.32 | async-start | bytes 2785280 | tf_op jit(solution)/shard_map/reduce_scatter | solution.py:316
  866.8 107.7 %reduce-scatter.55.cloned.1.call-start = ((), (), s32[]{:S(2)}) async-start(), calls=%async_computation.40 | async-start | bytes 589824
  876.7 39.8 %copy-start.13 = (bf16[2,272,1024]{2,1,0:T(8,128)(2,1)S(1)}, bf16[2,272,1024]{2,1,0:T(8,128)(2,1)}, u32[]{:S(2)}) copy-start(bf16[2,272,1024]{2,1,0:T(8,128)(2,1)} %param.14) | copy-start | bytes 3342340
  876.8 39.8 %copy-start.96 = (f32[1,1024]{1,0:T(1,128)S(1)}, f32[1,1024]{1,0:T(1,128)}, u32[]{:S(2)}) copy-start(f32[1,1024]{1,0:T(1,128)} %copy-done.95) | copy-start | bytes 12292
  876.8 39.8 %copy-start.115 = (f32[272]{0:T(512)S(1)}, f32[272]{0:T(512)}, u32[]{:S(2)}) copy-start(f32[272]{0:T(512)} %copy-done.114) | copy-start | bytes 3268
  876.8 39.8 %copy-start.117 = (f32[272]{0:T(512)S(1)}, f32[272]{0:T(512)}, u32[]{:S(2)}) copy-start(f32[272]{0:T(512)} %copy-done.116) | copy-start | bytes 3268
  876.8 39.8 %copy-start.120 = (f32[272]{0:T(512)S(1)}, f32[272]{0:T(512)}, u32[]{:S(2)}) copy-start(f32[272]{0:T(512)} %copy-done.119) | copy-start | bytes 3268
  876.8 39.8 %copy-start.122 = (f32[272]{0:T(512)S(1)}, f32[272]{0:T(512)}, u32[]{:S(2)}) copy-start(f32[272]{0:T(512)} %copy-done.121) | copy-start | bytes 3268
  876.8 113.0 %reduce-scatter.49.cloned.1.call-start = ((), (), s32[]{:S(2)}) async-start(), calls=%async_computation.37 | async-start | bytes 147456
  877.6 41.3 %copy-start.141 = (f32[1024]{0:T(1024)S(1)}, f32[1024]{0:T(1024)}, u32[]{:S(2)}) copy-start(f32[1024]{0:T(1024)} %get-tuple-element.18) | copy-start | bytes 12292
  877.6 41.3 %copy-start.142 = (f32[1024]{0:T(1024)S(1)}, f32[1024]{0:T(1024)}, u32[]{:S(2)}) copy-start(f32[1024]{0:T(1024)} %get-tuple-element.29) | copy-start | bytes 12292
  877.7 41.3 %copy-start.145 = (f32[1024]{0:T(1024)S(1)}, f32[1024]{0:T(1024)}, u32[]{:S(2)}) copy-start(f32[1024]{0:T(1024)} %get-tuple-element.16) | copy-start | bytes 12292
  877.7 41.3 %copy-start.146 = (f32[1024]{0:T(1024)S(1)}, f32[1024]{0:T(1024)}, u32[]{:S(2)}) copy-start(f32[1024]{0:T(1024)} %get-tuple-element.65) | copy-start | bytes 12292
  877.7 41.3 %copy-start.152 = (f32[1024]{0:T(1024)S(1)}, f32[1024]{0:T(1024)}, u32[]{:S(2)}) copy-start(f32[1024]{0:T(1024)} %get-tuple-element.26) | copy-start | bytes 12292
  877.7 41.3 %copy-start.153 = (f32[1024]{0:T(1024)S(1)}, f32[1024]{0:T(1024)}, u32[]{:S(2)}) copy-start(f32[1024]{0:T(1024)} %get-tuple-element.125) | copy-start | bytes 12292
  879.1 41.1 %copy-start.143 = (f32[1024]{0:T(1024)S(1)}, f32[1024]{0:T(1024)}, u32[]{:S(2)}) copy-start(f32[1024]{0:T(1024)} %get-tuple-element.39) | copy-start | bytes 12292
  879.1 41.1 %copy-start.144 = (f32[1024]{0:T(1024)S(1)}, f32[1024]{0:T(1024)}, u32[]{:S(2)}) copy-start(f32[1024]{0:T(1024)} %get-tuple-element.62) | copy-start | bytes 12292
  879.1 41.1 %copy-start.150 = (f32[1024]{0:T(1024)S(1)}, f32[1024]{0:T(1024)}, u32[]{:S(2)}) copy-start(f32[1024]{0:T(1024)} %get-tuple-element.51) | copy-start | bytes 12292
  879.1 41.1 %copy-start.151 = (f32[1024]{0:T(1024)S(1)}, f32[1024]{0:T(1024)}, u32[]{:S(2)}) copy-start(f32[1024]{0:T(1024)} %get-tuple-element.122) | copy-start | bytes 12292
  880.7 146.2 %reduce-scatter.51.cloned.1.call-start = ((), (), s32[]{:S(2)}) async-start(), calls=%async_computation.38 | async-start | bytes 589824
  920.1 144.3 %reduce-scatter.53.cloned.1.call-start = ((), (), s32[]{:S(2)}) async-start(), calls=%async_computation.39 | async-start | bytes 589824
  921.3 198.4 %reduce-scatter.47.cloned.1.call-start = ((), (), s32[]{:S(2)}) async-start(), calls=%async_computation.36 | async-start | bytes 4718592 | tf_op jit(solution)/shard_map/reduce_scatter | solution.py:341
  929.8 245.5 %reduce-scatter.45.cloned.1.call-start = ((), (), s32[]{:S(2)}) async-start(), calls=%async_computation.35 | async-start | bytes 4718592 | tf_op jit(solution)/shard_map/reduce_scatter | solution.py:339
  940.0 275.1 %reduce-scatter.43.cloned.1.call-start = ((), (), s32[]{:S(2)}) async-start(), calls=%async_computation.34 | async-start | bytes 1179648 | tf_op jit(solution)/shard_map/reduce_scatter | solution.py:338
  945.5 319.7 %reduce-scatter.41.cloned.1.call-start = ((), (), s32[]{:S(2)}) async-start(), calls=%async_computation.33 | async-start | bytes 3538944 | tf_op jit(solution)/shard_map/reduce_scatter | solution.py:336
  956.3 34.9 %copy-start.29 = (f32[272,1024]{1,0:T(8,128)S(1)}, f32[272,1024]{1,0:T(8,128)}, u32[]{:S(2)}) copy-start(f32[272,1024]{1,0:T(8,128)} %copy-done.28) | copy-start | bytes 3342340
  956.3 34.9 %copy-start.31 = (f32[272,1024]{1,0:T(8,128)S(1)}, f32[272,1024]{1,0:T(8,128)}, u32[]{:S(2)}) copy-start(f32[272,1024]{1,0:T(8,128)} %copy-done.30) | copy-start | bytes 3342340
  (163 other events, 628.7 us)
Sparse Core Ops, SparseCore 0:
  9.9 28.3 all-gather.13
  40.5 48.3 all-gather.19
  91.0 47.1 all-gather.11
  186.4 44.8 reduce-scatter.24
  233.4 45.4 reduce-scatter.28
  280.6 27.2 all-gather.15
  326.6 29.2 all-gather.17
  383.5 44.1 reduce-scatter.26
  430.0 45.4 reduce-scatter.30
  484.2 47.7 all-gather.25
  533.6 47.1 all-gather.21
  582.9 44.8 reduce-scatter.36
  630.1 45.4 reduce-scatter.32
  686.0 47.7 all-gather.23
  735.2 47.1 all-gather.27
  824.1 44.8 reduce-scatter.34
  871.1 45.4 reduce-scatter.38
  919.5 33.5 reduce-scatter.54
  956.4 33.3 reduce-scatter.48
  992.7 34.1 reduce-scatter.50
  1030.3 34.1 reduce-scatter.52
  1068.4 51.3 reduce-scatter.46
  1124.0 51.3 reduce-scatter.44
  1179.0 36.0 reduce-scatter.42
  1219.0 46.1 reduce-scatter.40
